TPU v7x, 256 devices: a whole 4x4x8 slice. The times are simulated.
256 devices in a mesh: mp: 32 (over z, y_hi, core), dp: 8 (over x, y_lo).
Axes of the slice: x: 4, y: 4 (y_hi: 2, y_lo: 2; y = y_hi * 2 + y_lo), z: 8, core: 2. Of those that a mesh axis runs over, the one named last changes fastest.
Arguments:
- tokens: bfloat16 [1024, 8192], P('mp', 'dp'), may hold values from -6 to 6
- gate_weight: bfloat16 [8192, 16384], P('dp', 'mp'), may hold values from -0.0625 to 0.0625
- up_weight: bfloat16 [8192, 16384], P('dp', 'mp'), may hold values from -0.0625 to 0.0625
- down_weight: bfloat16 [16384, 8192], P('mp', 'dp'), may hold values from -0.046875 to 0.046875
- cotangent: bfloat16 [1024, 8192], P('mp', 'dp'), may hold values from -6 to 6
Outputs:
- mixed: bfloat16 [1024, 8192], P('mp', 'dp')
- token_grad: bfloat16 [1024, 8192], P('mp', 'dp')
- gate_grad: bfloat16 [8192, 16384], P('dp', 'mp')
- up_grad: bfloat16 [8192, 16384], P('dp', 'mp')
- down_grad: bfloat16 [16384, 8192], P('mp', 'dp')
All inputs are finite; a program needn't handle non-finite values.
Results may differ from a plain program's by a relative error of at most 0.005.
Values may be sent and summed in bfloat16 or wider, within the bound.
No kernel may reach another device: no remote copies, remote signals or barrier semaphores. Data moves between devices by JAX's collectives and lax.ppermute only.
A program may use at most 64 MiB of HBM per device.

v0:
```python
import jax
import jax.numpy as jnp
from jax import lax
from jax.sharding import PartitionSpec as P


def contract_rows(left, right):
    return lax.dot_general(
        left, right, (((0,), (0,)), ((), ())), preferred_element_type=jnp.float32
    )


def contract_cols(left, right):
    return lax.dot_general(
        left, right, (((1,), (1,)), ((), ())), preferred_element_type=jnp.float32
    )


def body(tokens, gate_weight, up_weight, down_weight, cotangent):
    token_all = lax.all_gather(tokens, "mp", axis=0, tiled=True)
    width = gate_weight.shape[1]
    block = token_all
    first = jnp.dot(block, gate_weight, preferred_element_type=jnp.float32)
    second = jnp.dot(block, up_weight, preferred_element_type=jnp.float32)
    both = lax.psum(jnp.concatenate([first, second], axis=1), "dp")
    gate = both[:, :width]
    up = both[:, width:]
    sig = jax.nn.sigmoid(gate)
    act = gate * sig
    hidden_part = (act * up).astype(jnp.bfloat16)
    block = hidden_part
    mixed = lax.psum_scatter(
        jnp.dot(block, down_weight, preferred_element_type=jnp.float32),
        "mp",
        scatter_dimension=0,
        tiled=True,
    ).astype(jnp.bfloat16)
    cot_all = lax.all_gather(cotangent, "mp", axis=0, tiled=True)
    down_grad = contract_rows(hidden_part, cot_all).astype(jnp.bfloat16)
    block = cot_all
    hidden_back = lax.psum(contract_cols(block, down_weight), "dp")
    pre_gate = (hidden_back * up * sig * (1.0 + gate * (1.0 - sig))).astype(jnp.bfloat16)
    pre_up = (hidden_back * act).astype(jnp.bfloat16)
    gate_all, up_all = (pre_gate, pre_up)
    gate_grad = contract_rows(token_all, gate_all).astype(jnp.bfloat16)
    up_grad = contract_rows(token_all, up_all).astype(jnp.bfloat16)
    first = gate_all
    second = up_all
    token_grad = lax.psum_scatter(
        contract_cols(first, gate_weight) + contract_cols(second, up_weight),
        "mp",
        scatter_dimension=0,
        tiled=True,
    ).astype(jnp.bfloat16)
    return (mixed, token_grad, gate_grad, up_grad, down_grad)


def solution(mesh):
    in_specs = (P("mp", "dp"), P("dp", "mp"), P("dp", "mp"), P("mp", "dp"), P("mp", "dp"))
    out_specs = (P("mp", "dp"), P("mp", "dp"), P("dp", "mp"), P("dp", "mp"), P("mp", "dp"))
    return jax.shard_map(body, mesh=mesh, in_specs=in_specs, out_specs=out_specs, check_vma=False)
```

profile of v0, /device:TPU:6, one launch (start us, length us, event | category | flops | bytes accessed | tf_op | source)
XLA Modules:
  0.0 717.8 jit_solution(3119205423730051404)
XLA Ops:
  7.2 0.0 copy-start
  7.2 0.0 all-gather.3.cloned.1.call-start
  7.2 0.7 all-gather.3.cloned.1.call-update
  7.9 0.0 all-gather.5.cloned.1.call-start
  8.0 0.7 all-gather.5.cloned.1.call-update
  8.7 0.0 all-reduce.3.cloned.1.call-start
  8.7 84.9 %all-gather.3.cloned.1.call-done = bf16[1024,1024]{1,0:T(8,128)(2,1)} async-done(((bf16[32,1024]{1,0:T(8,128)(2,1)}), bf16[1024,1024]{1,0:T(8,128)(2,1)}) %all-gather.3.cloned.1.call-update) | async-done | bytes 2097168 | tf_op jit(solution)/shard_map/all_gather | solution.py:20
  93.6 0.0 copy-start.4
  93.6 3.3 fusion.4
  96.9 0.0 copy-done
  96.9 0.0 copy-done.4
  96.9 1.3 fusion.3
  98.2 0.0 copy-start.3
  98.2 2.5 pad_maximum_fusion
  100.7 72.0 %all-gather.5.cloned.1.call-done = bf16[1024,1024]{1,0:T(8,128)(2,1)} async-done(((bf16[32,1024]{1,0:T(8,128)(2,1)}), bf16[1024,1024]{1,0:T(8,128)(2,1)}) %all-gather.5.cloned.1.call-update) | async-done | bytes 2097168 | tf_op jit(solution)/shard_map/all_gather | solution.py:38
  172.7 0.0 copy-done.3
  172.7 4.2 fusion.6
  176.9 0.0 all-reduce.3.cloned.1.call-update
  176.9 0.0 reduce-scatter.5.cloned.1.call-start
  177.0 262.9 %all-reduce.3.cloned.1.call-done = (f32[1024,1024]{0,1:T(8,128)}, f32[1024,512]{0,1:T(8,128)}) async-done(((f32[1024,1024]{0,1:T(8,128)}, f32[1024,512]{0,1:T(8,128)}), (f32[1024,1024]{0,1:T(8,128)}, f32[1024,512]{0,1:T(8,128)})) %all-reduce.3.cloned.1.call-update) | async-done | bytes 6291472 | tf_op jit(solution)/shard_map/psum | solution.py:25
  439.9 4.3 multiply_convert_fusion
  444.2 0.0 copy-start.2
  444.2 0.0 copy-start.1
  444.2 1.3 fusion.7
  445.5 0.0 copy-done.2
  445.5 0.3 copy-done.1
  445.8 3.3 convolution_add_fusion
  449.1 0.0 reduce-scatter.5.cloned.1.call-update
  449.1 0.2 reduce-scatter.3.cloned.1.call-start
  449.3 4.5 fusion.5
  453.8 0.0 reduce-scatter.3.cloned.1.call-update
  453.8 4.1 fusion.1
  458.0 2.3 copy.11
  460.3 3.8 fusion.2
  464.1 2.3 copy.12
  466.4 3.9 convolution_convert_fusion
  470.2 109.2 %reduce-scatter.5.cloned.1.call-done = f32[32,1024]{1,0:T(8,128)} async-done(((f32[1024,1024]{1,0:T(8,128)}), f32[32,1024]{1,0:T(8,128)}) %reduce-scatter.5.cloned.1.call-update) | async-done | bytes 131088 | tf_op jit(solution)/shard_map/reduce_scatter | solution.py:49
  579.4 1.5 convert_element_type.34
  581.0 128.8 %reduce-scatter.3.cloned.1.call-done = f32[32,1024]{1,0:T(8,128)} async-done(((f32[1024,1024]{1,0:T(8,128)}), f32[32,1024]{1,0:T(8,128)}) %reduce-scatter.3.cloned.1.call-update) | async-done | bytes 131088 | tf_op jit(solution)/shard_map/reduce_scatter | solution.py:32
  709.8 1.5 convert_element_type.31
Async XLA Ops:
  7.2 89.7 %copy-start = (bf16[1024,512]{1,0:T(8,128)(2,1)S(1)}, bf16[1024,512]{1,0:T(8,128)(2,1)}, u32[]{:S(2)}) copy-start(bf16[1024,512]{1,0:T(8,128)(2,1)} %param.6) | copy-start | bytes 3145732
  7.2 86.4 %all-gather.3.cloned.1.call-start = ((), (), s32[]{:S(2)}) async-start(), calls=%async_computation.2 | async-start | bytes 2162688 | tf_op jit(solution)/shard_map/all_gather | solution.py:20
  7.9 164.8 %all-gather.5.cloned.1.call-start = ((), (), s32[]{:S(2)}) async-start(), calls=%async_computation.4 | async-start | bytes 2162688 | tf_op jit(solution)/shard_map/all_gather | solution.py:38
  8.7 431.2 %all-reduce.3.cloned.1.call-start = ((), (), s32[]{:S(2)}) async-start(), calls=%async_computation.6 | async-start | bytes 12582912 | tf_op jit(solution)/shard_map/psum | solution.py:25
  93.6 3.3 copy-start.4
  98.2 74.5 %copy-start.3 = (bf16[512,1024]{1,0:T(8,128)(2,1)S(1)}, bf16[512,1024]{1,0:T(8,128)(2,1)}, u32[]{:S(2)}) copy-start(bf16[512,1024]{1,0:T(8,128)(2,1)} %param.8) | copy-start | bytes 3145732
  176.9 402.5 %reduce-scatter.5.cloned.1.call-start = ((), (), s32[]{:S(2)}) async-start(), calls=%async_computation.5 | async-start | bytes 4325376 | tf_op jit(solution)/shard_map/reduce_scatter | solution.py:49
  444.2 1.3 copy-start.2
  444.2 1.6 copy-start.1
  449.1 260.7 %reduce-scatter.3.cloned.1.call-start = ((), (), s32[]{:S(2)}) async-start(), calls=%async_computation.3 | async-start | bytes 4325376 | tf_op jit(solution)/shard_map/reduce_scatter | solution.py:32
Sparse Core Ops, SparseCore 0:
  10.8 82.7 all-gather.2
  96.4 76.3 all-gather.4
  177.1 262.8 all-reduce.2
  449.2 130.1 reduce-scatter.4
  583.5 126.2 reduce-scatter.2
where the time goes:
time: 718 us
  waiting for transfers between devices  659 us (92%)
  matrix products  29.7 us (4%)
  between operations  13.9 us (2%)
  other arithmetic  9.84 us (1%)
    psum x1, waiting for transfers between devices, body(): both = lax.psum(jnp.concatenate([first, second], axis=1), 'dp')  263 us
    reduce_scatter x1, waiting for transfers between devices, body(): lax.psum_scatter(jnp.dot(block, down_weight, preferred_element_type=jnp.f...  129 us
    reduce_scatter x1, waiting for transfers between devices, body(): lax.psum_scatter(contract_cols(first, gate_weight) + contract_cols(second...  109 us
    all_gather x1, waiting for transfers between devices, body(): token_all = lax.all_gather(tokens, 'mp', axis=0, tiled=True)  84.9 us
    all_gather x1, waiting for transfers between devices, body(): cot_all = lax.all_gather(cotangent, 'mp', axis=0, tiled=True)  72 us
  transfers between devices with their start and end apart: 5, of which 5 were waited for; matrix products, arithmetic and copies ran while one was open for 4% of the time, Pallas kernels for 0%

commit v1 on v0

--- a/solution.py
+++ b/solution.py
@@ -22,7 +22,7 @@
     block = token_all
     first = jnp.dot(block, gate_weight, preferred_element_type=jnp.float32)
     second = jnp.dot(block, up_weight, preferred_element_type=jnp.float32)
-    both = lax.psum(jnp.concatenate([first, second], axis=1), "dp")
+    both = jnp.sum(lax.all_gather(jnp.concatenate([first, second], axis=1), "dp"), axis=0)
     gate = both[:, :width]
     up = both[:, width:]
     sig = jax.nn.sigmoid(gate)

time: 718 us -> 1200 us (1.67)
  waiting for transfers between devices: 659 us -> 1090 us
  local copies, waits for them, and re-layouts: 4.87 us -> 48.6 us
  other arithmetic: 9.84 us -> 22.5 us
    all_gather x0 -> x1, waiting for transfers between devices: none -> 637 us  [body(): lax.all_gather(jnp.concatenate([first, second], axis=1), 'dp')]
    psum x1, waiting for transfers between devices: 263 us -> 56.6 us  [body(): hidden_back = lax.psum(contract_cols(block, down_weight), 'dp')]
    unnamed x12 -> x17, local copies, waits for them, and re-layouts: 4.87 us -> 44.5 us
    reduce_sum x0 -> x1, other arithmetic: none -> 12.6 us  [body(): jnp.sum(lax.all_gather(jnp.concatenate([first, second], axis=1), 'dp'), a...]
  transfers between devices with their start and end apart: 5 -> 6, of which waited for: 5 -> 6; matrix products, arithmetic and copies ran while one was open for 4% -> 7% of each run, Pallas kernels for 0% -> 0%
where the time goes in v1:
time: 1200 us
  waiting for transfers between devices  1090 us (91%)
  local copies, waits for them, and re-layouts  48.6 us (4%)
  matrix products  29.5 us (2%)
  other arithmetic  22.5 us (2%)
  between operations  14.2 us (1%)
    all_gather x1, waiting for transfers between devices, body(): lax.all_gather(jnp.concatenate([first, second], axis=1), 'dp')  637 us
    reduce_scatter x1, waiting for transfers between devices, body(): lax.psum_scatter(jnp.dot(block, down_weight, preferred_element_type=jnp.f...  129 us
    reduce_scatter x1, waiting for transfers between devices, body(): lax.psum_scatter(contract_cols(first, gate_weight) + contract_cols(second...  108 us
    all_gather x1, waiting for transfers between devices, body(): token_all = lax.all_gather(tokens, 'mp', axis=0, tiled=True)  84.9 us
    all_gather x1, waiting for transfers between devices, body(): cot_all = lax.all_gather(cotangent, 'mp', axis=0, tiled=True)  72.1 us
    psum x1, waiting for transfers between devices, body(): hidden_back = lax.psum(contract_cols(block, down_weight), 'dp')  56.6 us
    unnamed x17, local copies, waits for them, and re-layouts  44.5 us
  transfers between devices with their start and end apart: 6, of which 6 were waited for; matrix products, arithmetic and copies ran while one was open for 7% of the time, Pallas kernels for 0%

profile of v1, /device:TPU:6, one launch (start us, length us, event | category | flops | bytes accessed | tf_op | source)
XLA Modules:
  0.0 1203.9 jit_solution(17300734887827706169)
XLA Ops:
  7.2 0.0 copy-start
  7.2 0.0 all-gather.5.cloned.1.call-start
  7.2 0.7 all-gather.5.cloned.1.call-update
  7.9 0.0 all-gather.7.cloned.1.call-start
  8.0 0.7 all-gather.7.cloned.1.call-update
  8.7 0.0 copy-start.3
  8.7 0.0 all-gather.9.cloned.1.call-start
  8.7 84.9 %all-gather.5.cloned.1.call-done = bf16[1024,1024]{1,0:T(8,128)(2,1)} async-done(((bf16[32,1024]{1,0:T(8,128)(2,1)}), bf16[1024,1024]{1,0:T(8,128)(2,1)}) %all-gather.5.cloned.1.call-update) | async-done | bytes 2097168 | tf_op jit(solution)/shard_map/all_gather | solution.py:20
  93.6 0.0 copy-done
  93.6 0.0 copy-start.1
  93.6 3.0 fusion.4
  96.6 0.0 copy-done.3
  96.6 0.0 copy-done.1
  96.6 1.3 fusion.5
  98.0 2.6 pad_maximum_fusion
  100.6 0.0 copy-start.5
  100.6 0.0 all-gather.9.cloned.1.call-update
  100.6 0.0 all-reduce.2.cloned.1.call-start
  100.6 72.1 %all-gather.7.cloned.1.call-done = bf16[1024,1024]{1,0:T(8,128)(2,1)} async-done(((bf16[32,1024]{1,0:T(8,128)(2,1)}), bf16[1024,1024]{1,0:T(8,128)(2,1)}) %all-gather.7.cloned.1.call-update) | async-done | bytes 2097168 | tf_op jit(solution)/shard_map/all_gather | solution.py:38
  172.7 0.0 copy-done.5
  172.7 4.2 fusion.7
  176.9 0.0 all-reduce.2.cloned.1.call-update
  176.9 0.2 reduce-scatter.5.cloned.1.call-start
  177.2 636.6 %all-gather.9.cloned.1.call-done = f32[8192,1024]{0,1:T(8,128)} async-done(((f32[1024,1024]{0,1:T(8,128)}), f32[8192,1024]{0,1:T(8,128)}) %all-gather.9.cloned.1.call-update) | async-done | bytes 33554448 | tf_op jit(solution)/shard_map/all_gather | solution.py:25
  813.8 34.9 %copy.18 = f32[128,8,8,1024]{3,2,1,0:T(8,128)S(1)} copy(f32[128,8,8,1024]{3,1,2,0:T(8,128)} %bitcast.27) | data formatting | bytes 67108864
  848.7 12.6 %bitcast_reduce_fusion = f32[1024,1024]{0,1:T(8,128)} fusion(f32[128,8,8,1024]{3,2,1,0:T(8,128)S(1)} %copy.18), kind=kLoop, calls=%fused_computation | loop fusion | flops 7340032 | bytes 37748736 | tf_op jit(solution)/shard_map/reduce_sum | solution.py:25
  861.3 4.0 fusion.3
  865.3 2.9 copy.16
  868.2 1.8 copy.17
  870.0 56.6 %all-reduce.2.cloned.1.call-done = f32[1024,512]{1,0:T(8,128)} async-done(((f32[1024,512]{1,0:T(8,128)}), f32[1024,512]{1,0:T(8,128)}) %all-reduce.2.cloned.1.call-update) | async-done | bytes 2097168 | tf_op jit(solution)/shard_map/psum | solution.py:41
  926.6 4.2 multiply_convert_fusion
  930.9 0.0 copy-start.2
  930.9 0.0 copy-start.4
  930.9 1.3 fusion.8
  932.2 0.0 copy-done.2
  932.2 0.3 copy-done.4
  932.5 3.3 convolution_add_fusion
  935.8 0.0 reduce-scatter.5.cloned.1.call-update
  935.8 0.3 reduce-scatter.3.cloned.1.call-start
  936.1 4.4 fusion.6
  940.5 0.0 reduce-scatter.3.cloned.1.call-update
  940.6 4.2 fusion.1
  944.7 2.3 copy.14
  947.0 3.9 fusion.2
  950.9 2.3 copy.15
  953.2 3.9 convolution_convert_fusion
  957.0 108.2 %reduce-scatter.5.cloned.1.call-done = f32[32,1024]{1,0:T(8,128)} async-done(((f32[1024,1024]{1,0:T(8,128)}), f32[32,1024]{1,0:T(8,128)}) %reduce-scatter.5.cloned.1.call-update) | async-done | bytes 131088 | tf_op jit(solution)/shard_map/reduce_scatter | solution.py:49
  1065.2 1.5 convert_element_type.34
  1066.7 128.8 %reduce-scatter.3.cloned.1.call-done = f32[32,1024]{1,0:T(8,128)} async-done(((f32[1024,1024]{1,0:T(8,128)}), f32[32,1024]{1,0:T(8,128)}) %reduce-scatter.3.cloned.1.call-update) | async-done | bytes 131088 | tf_op jit(solution)/shard_map/reduce_scatter | solution.py:32
  1195.5 1.5 convert_element_type.31
Async XLA Ops:
  7.2 86.4 %copy-start = (bf16[1024,512]{1,0:T(8,128)(2,1)S(1)}, bf16[1024,512]{1,0:T(8,128)(2,1)}, u32[]{:S(2)}) copy-start(bf16[1024,512]{1,0:T(8,128)(2,1)} %param.6) | copy-start | bytes 3145732
  7.2 86.4 %all-gather.5.cloned.1.call-start = ((), (), s32[]{:S(2)}) async-start(), calls=%async_computation.2 | async-start | bytes 2162688 | tf_op jit(solution)/shard_map/all_gather | solution.py:20
  7.9 164.8 %all-gather.7.cloned.1.call-start = ((), (), s32[]{:S(2)}) async-start(), calls=%async_computation.4 | async-start | bytes 2162688 | tf_op jit(solution)/shard_map/all_gather | solution.py:38
  8.7 88.0 %copy-start.3 = (bf16[1024,512]{1,0:T(8,128)(2,1)S(1)}, bf16[1024,512]{1,0:T(8,128)(2,1)}, u32[]{:S(2)}) copy-start(bf16[1024,512]{1,0:T(8,128)(2,1)} %param.7) | copy-start | bytes 3145732
  8.7 805.1 %all-gather.9.cloned.1.call-start = ((), (), s32[]{:S(2)}) async-start(), calls=%async_computation.7 | async-start | bytes 37748736 | tf_op jit(solution)/shard_map/all_gather | solution.py:25
  93.6 3.0 copy-start.1
  100.6 72.2 %copy-start.5 = (bf16[512,1024]{1,0:T(8,128)(2,1)S(1)}, bf16[512,1024]{1,0:T(8,128)(2,1)}, u32[]{:S(2)}) copy-start(bf16[512,1024]{1,0:T(8,128)(2,1)} %param.8) | copy-start | bytes 3145732
  100.6 826.1 %all-reduce.2.cloned.1.call-start = ((), (), s32[]{:S(2)}) async-start(), calls=%async_computation.5 | async-start | bytes 4194304 | tf_op jit(solution)/shard_map/psum | solution.py:41
  176.9 888.3 %reduce-scatter.5.cloned.1.call-start = ((), (), s32[]{:S(2)}) async-start(), calls=%async_computation.6 | async-start | bytes 4325376 | tf_op jit(solution)/shard_map/reduce_scatter | solution.py:49
  930.9 1.3 copy-start.2
  930.9 1.6 copy-start.4
  935.8 259.7 %reduce-scatter.3.cloned.1.call-start = ((), (), s32[]{:S(2)}) async-start(), calls=%async_computation.3 | async-start | bytes 4325376 | tf_op jit(solution)/shard_map/reduce_scatter | solution.py:32
Sparse Core Ops, SparseCore 0:
  10.8 82.7 all-gather.4
  96.4 76.3 all-gather.6
  174.5 639.2 all-gather.8
  816.3 110.2 all-reduce.1
  936.0 129.1 reduce-scatter.4
  1069.3 126.1 reduce-scatter.2
